TPU v7x, 32 devices: a whole 2x2x4 slice. The times are simulated.
32 devices in a mesh: row: 8 (over y, x, core), col: 4 (over z).
Axes of the slice: x: 2, y: 2, z: 4, core: 2. Of those that a mesh axis runs over, the one named last changes fastest.
Arguments:
- final_amp: bfloat16 [8, 32, 128, 440], P('row', 'col'), may hold values from -0.19921875 to 0.19921875
- initial_amp: bfloat16 [4, 32, 128, 440], P('col', 'row'), may hold values from -0.19921875 to 0.19921875
- pair_final: int32 [8, 4, 128], P('row', 'col'), may hold values from 0 to 31
- pair_initial: int32 [8, 4, 128], P('row', 'col'), may hold values from 0 to 31
- map_final: int32 [8, 32, 440], P('row', 'col'), may hold values from 0 to 439, each once within a row
- map_initial: int32 [4, 32, 440], P('col', 'row'), may hold values from 0 to 439, each once within a row
- counts: int32 [8, 4], P('row', 'col'), may hold values from 16 to 128, as said below
Outputs:
- density: float32 [440, 440], replicated
Inputs may be any that keep to these rules, and one draw needn't show every extreme that they name: `counts`: slots at or past a cell's count are ignored. Exactly one cell of every draw has 128 live slots.
All inputs are finite; a program needn't handle non-finite values.
Results may differ from a plain program's by a relative error of at most 0.0003.
Values may be sent and summed in bfloat16 or wider, within the bound.
A program may use at most 64 MiB of HBM per device.

v0:
```python
import jax
import jax.numpy as jnp
from jax import lax
from jax.sharding import PartitionSpec as P

GROUP = 32


def permute_columns(blocks, orbital_map):
    return jnp.take(blocks, orbital_map, axis=1)


def shards(final_amp, initial_amp, pair_final, pair_initial, map_final, map_initial, counts):
    own_final = jax.vmap(permute_columns)(final_amp[0], map_final[0])[None]
    own_initial = jax.vmap(permute_columns)(initial_amp[0], map_initial[0])[None]
    row_seg = lax.all_gather(own_final, "col", axis=1, tiled=True)[0]
    column_seg = lax.all_gather(own_initial, "row", axis=1, tiled=True)[0]
    slots_final = pair_final[0, 0]
    slots_initial = pair_initial[0, 0]
    live_count = counts[0, 0]
    orbitals = final_amp.shape[3]
    group_size = GROUP

    def advance(index, summed):
        first_slot = index * group_size
        which_final = lax.dynamic_slice_in_dim(slots_final, first_slot, group_size)
        which_initial = lax.dynamic_slice_in_dim(slots_initial, first_slot, group_size)
        live_mask = first_slot + jnp.arange(group_size, dtype=jnp.int32) < live_count
        left = jnp.take(row_seg, which_final, axis=0)
        right = jnp.take(column_seg, which_initial, axis=0)
        left = jnp.where(live_mask[:, None, None], left, jnp.zeros_like(left))
        product = lax.dot_general(
            left.reshape(-1, orbitals),
            right.reshape(-1, orbitals),
            (((0,), (0,)), ((), ())),
            preferred_element_type=jnp.float32,
        )
        return summed + product

    turns = (live_count + group_size - 1) // group_size
    partial_density = lax.fori_loop(0, turns, advance, jnp.zeros((orbitals, orbitals), jnp.float32))
    band = lax.psum_scatter(partial_density, "col", scatter_dimension=0, tiled=True)
    band = lax.psum(band, "row")
    density = lax.all_gather(band, "col", axis=0, tiled=True)
    return density


def solution(mesh):
    placed = (
        P("row", "col", None, None),
        P("col", "row", None, None),
        P("row", "col", None),
        P("row", "col", None),
        P("row", "col", None),
        P("col", "row", None),
        P("row", "col"),
    )
    return jax.shard_map(shards, mesh=mesh, in_specs=placed, out_specs=P(), check_vma=False)
```

profile of v0, /device:TPU:0, one launch (start us, length us, event | category | flops | bytes accessed | tf_op | source)
XLA Modules:
  0.0 321.1 jit_solution(12124861493017973160)
XLA Ops:
  6.5 0.8 fusion.18
  7.3 0.7 compare_and_fusion.2
  8.2 30.8 %gather_fusion.2 = bf16[3520,128]{1,0:T(8,128)(2,1)S(1)} fusion(bf16[8,128,440]{1,2,0:T(8,128)(2,1)S(1)} %bitcast.44, s32[3520]{0:T(1024)S(1)} %reshape.110), kind=kCustom, calls=%fused_computation.2 | custom fusion | bytes 1830400 | tf_op jit(solution)/shard_map/vmap(jit(_take))/gather | solution.py:10
  39.0 1.4 broadcast_select_fusion
  40.5 15.7 %gather_fusion.3 = bf16[1760,128]{1,0:T(8,128)(2,1)S(1)} fusion(bf16[4,128,440]{1,2,0:T(8,128)(2,1)S(1)} %bitcast.45, s32[1760]{0:T(1024)S(1)} %reshape.116), kind=kCustom, calls=%fused_computation.3 | custom fusion | bytes 915200 | tf_op jit(solution)/shard_map/vmap(jit(_take))/gather | solution.py:10
  56.3 1.1 broadcast_select_fusion.1
  58.2 56.1 %all-gather.4.cloned.1.call-done = bf16[1,32,128,440]{2,3,0,1:T(8,128)(2,1)} async-done(((bf16[1,8,128,440]{2,3,0,1:T(8,128)(2,1)}), bf16[1,32,128,440]{2,3,0,1:T(8,128)(2,1)}) %all-gather.4.cloned.1.call-update) | async-done | bytes 3604496 | tf_op jit(solution)/shard_map/all_gather | solution.py:16
  114.3 6.4 %copy.18 = bf16[32,128,440]{2,1,0:T(8,128)(2,1)} copy(bf16[32,128,440]{1,2,0:T(8,128)(2,1)} %bitcast.47) | data formatting | bytes 7208960 | tf_op jit(solution)/shard_map/while | solution.py:41
  120.7 28.2 %all-gather.6.cloned.1.call-done = bf16[1,32,128,440]{2,3,0,1:T(8,128)(2,1)} async-done(((bf16[1,4,128,440]{2,3,0,1:T(8,128)(2,1)}), bf16[1,32,128,440]{2,3,0,1:T(8,128)(2,1)}) %all-gather.6.cloned.1.call-update) | async-done | bytes 3604496 | tf_op jit(solution)/shard_map/all_gather | solution.py:17
  148.9 6.5 %copy.19 = bf16[32,128,440]{2,1,0:T(8,128)(2,1)} copy(bf16[32,128,440]{1,2,0:T(8,128)(2,1)} %bitcast.48) | data formatting | bytes 7208960 | tf_op jit(solution)/shard_map/while | solution.py:41
  155.5 33.5 %while.10 = (s32[]{:T(128)}, f32[440,440]{1,0:T(8,128)S(1)}, s32[]{:T(128)}, s32[]{:T(128)}, s32[128]{0:T(128)S(1)}, /*index=5*/bf16[32,128,440]{2,1,0:T(8,128)(...) while((s32[]{:T(128)}, f32[440,440]{1,0:T(8,128)S(1)}, ...), condition=%wide.region_1.3_spmd, body=%wide.region_0.0_spmd.sunk | while | flops 1591574016 | bytes 23185264 | solution.py:41
  155.6 5.0 %gather_fusion = bf16[32,128,440]{2,1,0:T(8,128)(2,1)} fusion(bf16[32,128,440]{2,1,0:T(8,128)(2,1)} %get-tuple-element.169, s32[1024]{0:T(1024)S(1)} %pad_clamp_fusion.4), kind=kCustom, calls=%fused_computation.1.clone.clone.1 | custom fusion | bytes 7209088 | tf_op jit(solution)/shard_map/while/body/jit(_take)/gather | solution.py:30
  160.6 4.9 %gather_fusion.1 = bf16[32,128,440]{2,1,0:T(8,128)(2,1)} fusion(bf16[32,128,440]{2,1,0:T(8,128)(2,1)} %get-tuple-element.167, s32[1024]{0:T(1024)S(1)} %pad_clamp_fusion.5), kind=kCustom, calls=%fused_computation.clone.clone.1 | custom fusion | bytes 7209088 | tf_op jit(solution)/shard_map/while/body/jit(_take)/gather | solution.py:29
  166.1 6.1 %fusion.25 = f32[440,440]{1,0:T(8,128)S(1)} fusion(f32[440,440]{1,0:T(8,128)S(1)} %get-tuple-element.151, bf16[32,128,440]{2,1,0:T(8,128)(2,1)} %gather_fusion, pred[32]{0:T(512)(128)(4,1)S(1)} %get-tuple-element.135, bf16[32,128,440]{2,1,0:T(8,128)(2,1)} %gather_fusion.1, pred[32]{0:T(512)(128)(4,1)S(1)} %get-tuple-element.137, ...), kind=kOutput, calls=%fused_computation.13.clone.1 | convolution fusion | flops 1591571456 | bytes 8757856 | tf_op jit(solution)/shard_map/while/body/dot_general | solution.py:32
  172.3 5.0 %gather_fusion = bf16[32,128,440]{2,1,0:T(8,128)(2,1)} fusion(bf16[32,128,440]{2,1,0:T(8,128)(2,1)} %get-tuple-element.169, s32[1024]{0:T(1024)S(1)} %pad_clamp_fusion.4), kind=kCustom, calls=%fused_computation.1.clone.clone.1 | custom fusion | bytes 7209088 | tf_op jit(solution)/shard_map/while/body/jit(_take)/gather | solution.py:30
  177.3 4.9 %gather_fusion.1 = bf16[32,128,440]{2,1,0:T(8,128)(2,1)} fusion(bf16[32,128,440]{2,1,0:T(8,128)(2,1)} %get-tuple-element.167, s32[1024]{0:T(1024)S(1)} %pad_clamp_fusion.5), kind=kCustom, calls=%fused_computation.clone.clone.1 | custom fusion | bytes 7209088 | tf_op jit(solution)/shard_map/while/body/jit(_take)/gather | solution.py:29
  182.9 6.1 %fusion.25 = f32[440,440]{1,0:T(8,128)S(1)} fusion(f32[440,440]{1,0:T(8,128)S(1)} %get-tuple-element.151, bf16[32,128,440]{2,1,0:T(8,128)(2,1)} %gather_fusion, pred[32]{0:T(512)(128)(4,1)S(1)} %get-tuple-element.135, bf16[32,128,440]{2,1,0:T(8,128)(2,1)} %gather_fusion.1, pred[32]{0:T(512)(128)(4,1)S(1)} %get-tuple-element.137, ...), kind=kOutput, calls=%fused_computation.13.clone.1 | convolution fusion | flops 1591571456 | bytes 8757856 | tf_op jit(solution)/shard_map/while/body/dot_general | solution.py:32
  188.9 22.8 %fusion = f32[112,440]{1,0:T(8,128)S(1)} fusion(f32[440,440]{1,0:T(8,128)S(1)} %get-tuple-element.49), kind=kCustom, calls=%all-reduce-scatter | all-reduce-scatter fusion | flops 197121 | bytes 972032
  211.7 2.1 collective-permute-start
  215.6 0.7 constant_dynamic-slice_fusion
  216.3 74.9 %all-reduce.4.cloned.1.call-done = f32[110,440]{1,0:T(8,128)} async-done(((f32[110,440]{1,0:T(8,128)}), f32[110,440]{1,0:T(8,128)}) %all-reduce.4.cloned.1.call-update) | async-done | bytes 193616 | tf_op jit(solution)/shard_map/psum | solution.py:43
  291.2 1.1 copy.20
  292.3 20.9 %all-gather = f32[4,110,440]{1,2,0:T(8,128)S(1)} all-gather(f32[1,110,440]{1,2,0:T(8,128)S(1)} %copy.20), channel_id=1, replica_groups=mesh['row'=8,'col'=4] {'col'}, dimensions={0}, use_global_device_ids=true | all-gather | bytes 968000 | tf_op jit(solution)/shard_map/all_gather | solution.py:44
  313.6 1.0 reshape.125
  (36 shorter events, 3.3 us)
Async XLA Ops:
  6.5 1.6 copy-start
  6.5 107.7 %all-gather.4.cloned.1.call-start = ((), (), s32[]{:S(2)}) async-start(), calls=%async_computation | async-start | bytes 4505600 | tf_op jit(solution)/shard_map/all_gather | solution.py:16
  8.2 32.3 %copy-start.2 = (s32[1,4,440]{2,1,0:T(4,128)S(1)}, s32[1,4,440]{2,1,0:T(4,128)}, u32[]{:S(2)}) copy-start(s32[1,4,440]{2,1,0:T(4,128)} %param.16) | copy-start | bytes 21124
  8.2 32.4 %copy-start.1 = (bf16[1,4,128,440]{2,3,1,0:T(8,128)(2,1)S(1)}, bf16[1,4,128,440]{2,3,1,0:T(8,128)(2,1)}, u32[]{:S(2)}) copy-start(bf16[1,4,128,440]{2,3,1,0:T(8,128)(2,1)} %param.12) | copy-start | bytes 1351684
  40.4 108.5 %all-gather.6.cloned.1.call-start = ((), (), s32[]{:S(2)}) async-start(), calls=%async_computation.1 | async-start | bytes 4055040 | tf_op jit(solution)/shard_map/all_gather | solution.py:17
  57.4 233.8 %all-reduce.4.cloned.1.call-start = ((), (), s32[]{:S(2)}) async-start(), calls=%async_computation.2 | async-start | bytes 458752 | tf_op jit(solution)/shard_map/psum | solution.py:43
  148.9 6.6 %copy-start.3 = (s32[1,1,128]{2,1,0:T(1,128)S(1)}, s32[1,1,128]{2,1,0:T(1,128)}, u32[]{:S(2)}) copy-start(s32[1,1,128]{2,1,0:T(1,128)} %param.13) | copy-start | bytes 1540
  148.9 6.6 %copy-start.4 = (s32[1,1,128]{2,1,0:T(1,128)S(1)}, s32[1,1,128]{2,1,0:T(1,128)}, u32[]{:S(2)}) copy-start(s32[1,1,128]{2,1,0:T(1,128)} %param.14) | copy-start | bytes 1540
  155.5 58.4 %copy-start.5 = (u32[32]{0:T(128)S(1)}, u32[32]{0:T(128)}, u32[]{:S(2)}) copy-start(u32[32]{0:T(128)} %constant.104) | copy-start | bytes 388
  211.7 3.6 %collective-permute-start = (f32[6,440]{1,0:T(8,128)S(1)}, f32[6,440]{1,0:T(8,128)S(1)}, u32[]{:S(2)}, u32[]{:S(2)}) collective-permute-start(f32[6,440]{1,0:T(8,128)S(1)} %slice.8), channel_id=1, source_target_pairs={{0,1},{1,2},{2,3},{4,5},{5,6},{6,7},{8,9},{9,10},{10,11},{12,13},{... | collective-permute-start | bytes 31688
Sparse Core Ops, SparseCore 0:
  40.5 73.7 all-gather.3
  116.2 32.6 all-gather.5
  216.4 74.7 all-reduce.3
where the time goes:
time: 322 us; the launch traced here: 321 us
  waiting for transfers between devices  159 us (49%)
  local copies, waits for them, and re-layouts  83.4 us (26%)
  blocking collectives  43.7 us (14%)
  between operations  14.6 us (5%)
  matrix products  12.1 us (4%)
  other arithmetic  5.57 us (2%)
    psum x1, waiting for transfers between devices, shards(): band = lax.psum(band, 'row')  74.9 us
    all_gather x1, waiting for transfers between devices, shards(): row_seg = lax.all_gather(own_final, 'col', axis=1, tiled=True)[0]  56.1 us
    gather x4, local copies, waits for them, and re-layouts, permute_columns(): return jnp.take(blocks, orbital_map, axis=1)  46.6 us
    all_gather x1, waiting for transfers between devices, shards(): column_seg = lax.all_gather(own_initial, 'row', axis=1, tiled=True)[0]  28.2 us
    unnamed x1, blocking collectives  22.8 us
    all_gather x1, blocking collectives, shards(): density = lax.all_gather(band, 'col', axis=0, tiled=True)  20.9 us
    while x2, local copies, waits for them, and re-layouts, shards(): lax.fori_loop(0, turns, advance, jnp.zeros((orbitals, orbitals), jnp.floa...  12.9 us
    dot_general x2, matrix products, advance(): lax.dot_general(left.reshape(-1, orbitals), right.reshape(-1, orbitals),...  12.1 us
  transfers between devices with their start and end apart: 4, of which 4 were waited for; matrix products, arithmetic and copies ran while one was open for 7% of the time, Pallas kernels for 0%

commit v1 on v0

--- a/solution.py
+++ b/solution.py
@@ -41,7 +41,12 @@
     partial_density = lax.fori_loop(0, turns, advance, jnp.zeros((orbitals, orbitals), jnp.float32))
     band = lax.psum_scatter(partial_density, "col", scatter_dimension=0, tiled=True)
     band = lax.psum(band, "row")
-    density = lax.all_gather(band, "col", axis=0, tiled=True)
+    ring = [band]
+    for hop in range(3):
+        ring.append(lax.ppermute(ring[-1], "col", [(dev, (dev + 1) % 4) for dev in range(4)]))
+    density = jnp.roll(
+        jnp.concatenate(ring[::-1], axis=0), (lax.axis_index("col") + 1) * ring[0].shape[0], axis=0
+    )
     return density
 
 

time: 322 us -> 330 us (1.025)
  waiting for transfers between devices: 159 us -> 185 us
  blocking collectives: 43.7 us -> 22.8 us
    ppermute x0 -> x3, waiting for transfers between devices: none -> 25.4 us  [shards(): lax.ppermute(ring[-1], 'col', [(dev, (dev + 1) % 4) for dev in range(4)])]
    all_gather x1 -> x0, blocking collectives: 20.9 us -> none  [shards(): density = lax.all_gather(band, 'col', axis=0, tiled=True)]
  transfers between devices with their start and end apart: 4 -> 7, of which waited for: 4 -> 7; matrix products, arithmetic and copies ran while one was open for 7% -> 7% of each run, Pallas kernels for 0% -> 0%
where the time goes in v1:
time: 330 us; the launch traced here: 329 us
  waiting for transfers between devices  185 us (56%)
  local copies, waits for them, and re-layouts  85.1 us (26%)
  blocking collectives  22.8 us (7%)
  between operations  14.6 us (4%)
  matrix products  12.1 us (4%)
  other arithmetic  5.57 us (2%)
  starting transfers between devices  3.7 us (1%)
    psum x1, waiting for transfers between devices, shards(): band = lax.psum(band, 'row')  74.9 us
    all_gather x1, waiting for transfers between devices, shards(): row_seg = lax.all_gather(own_final, 'col', axis=1, tiled=True)[0]  56.1 us
    gather x4, local copies, waits for them, and re-layouts, permute_columns(): return jnp.take(blocks, orbital_map, axis=1)  46.6 us
    all_gather x1, waiting for transfers between devices, shards(): column_seg = lax.all_gather(own_initial, 'row', axis=1, tiled=True)[0]  28.2 us
    ppermute x3, waiting for transfers between devices, shards(): lax.ppermute(ring[-1], 'col', [(dev, (dev + 1) % 4) for dev in range(4)])  25.4 us
    unnamed x1, blocking collectives  22.8 us
    while x2, local copies, waits for them, and re-layouts, shards(): lax.fori_loop(0, turns, advance, jnp.zeros((orbitals, orbitals), jnp.floa...  12.9 us
    dot_general x2, matrix products, advance(): lax.dot_general(left.reshape(-1, orbitals), right.reshape(-1, orbitals),...  12.1 us
  transfers between devices with their start and end apart: 7, of which 7 were waited for; matrix products, arithmetic and copies ran while one was open for 7% of the time, Pallas kernels for 0%

profile of v1, /device:TPU:0, one launch (start us, length us, event | category | flops | bytes accessed | tf_op | source)
XLA Modules:
  0.0 328.7 jit_solution(8888139109966720143)
XLA Ops:
  8.2 30.8 %gather_fusion.2 = bf16[3520,128]{1,0:T(8,128)(2,1)S(1)} fusion(bf16[8,128,440]{1,2,0:T(8,128)(2,1)S(1)} %bitcast.43, s32[3520]{0:T(1024)S(1)} %reshape.110), kind=kCustom, calls=%fused_computation.2 | custom fusion | bytes 1830400 | tf_op jit(solution)/shard_map/vmap(jit(_take))/gather | solution.py:10
  39.0 1.4 broadcast_select_fusion
  40.5 15.7 %gather_fusion.3 = bf16[1760,128]{1,0:T(8,128)(2,1)S(1)} fusion(bf16[4,128,440]{1,2,0:T(8,128)(2,1)S(1)} %bitcast.44, s32[1760]{0:T(1024)S(1)} %reshape.116), kind=kCustom, calls=%fused_computation.3 | custom fusion | bytes 915200 | tf_op jit(solution)/shard_map/vmap(jit(_take))/gather | solution.py:10
  56.3 1.1 broadcast_select_fusion.1
  58.2 56.1 %all-gather.3.cloned.1.call-done = bf16[1,32,128,440]{2,3,0,1:T(8,128)(2,1)} async-done(((bf16[1,8,128,440]{2,3,0,1:T(8,128)(2,1)}), bf16[1,32,128,440]{2,3,0,1:T(8,128)(2,1)}) %all-gather.3.cloned.1.call-update) | async-done | bytes 3604496 | tf_op jit(solution)/shard_map/all_gather | solution.py:16
  114.3 6.4 %copy.14 = bf16[32,128,440]{2,1,0:T(8,128)(2,1)} copy(bf16[32,128,440]{1,2,0:T(8,128)(2,1)} %bitcast.46) | data formatting | bytes 7208960 | tf_op jit(solution)/shard_map/while | solution.py:41
  120.7 28.2 %all-gather.5.cloned.1.call-done = bf16[1,32,128,440]{2,3,0,1:T(8,128)(2,1)} async-done(((bf16[1,4,128,440]{2,3,0,1:T(8,128)(2,1)}), bf16[1,32,128,440]{2,3,0,1:T(8,128)(2,1)}) %all-gather.5.cloned.1.call-update) | async-done | bytes 3604496 | tf_op jit(solution)/shard_map/all_gather | solution.py:17
  148.9 6.5 %copy.15 = bf16[32,128,440]{2,1,0:T(8,128)(2,1)} copy(bf16[32,128,440]{1,2,0:T(8,128)(2,1)} %bitcast.47) | data formatting | bytes 7208960 | tf_op jit(solution)/shard_map/while | solution.py:41
  155.5 33.5 %while.10 = (s32[]{:T(128)}, f32[440,440]{1,0:T(8,128)S(1)}, s32[]{:T(128)}, s32[]{:T(128)}, s32[128]{0:T(128)S(1)}, /*index=5*/bf16[32,128,440]{2,1,0:T(8,128)(...) while((s32[]{:T(128)}, f32[440,440]{1,0:T(8,128)S(1)}, ...), condition=%wide.region_1.3_spmd, body=%wide.region_0.0_spmd.sunk | while | flops 1591574016 | bytes 23185264 | solution.py:41
  155.6 5.0 %gather_fusion = bf16[32,128,440]{2,1,0:T(8,128)(2,1)} fusion(bf16[32,128,440]{2,1,0:T(8,128)(2,1)} %get-tuple-element.169, s32[1024]{0:T(1024)S(1)} %pad_clamp_fusion.4), kind=kCustom, calls=%fused_computation.1.clone.clone.1 | custom fusion | bytes 7209088 | tf_op jit(solution)/shard_map/while/body/jit(_take)/gather | solution.py:30
  160.6 4.9 %gather_fusion.1 = bf16[32,128,440]{2,1,0:T(8,128)(2,1)} fusion(bf16[32,128,440]{2,1,0:T(8,128)(2,1)} %get-tuple-element.167, s32[1024]{0:T(1024)S(1)} %pad_clamp_fusion.5), kind=kCustom, calls=%fused_computation.clone.clone.1 | custom fusion | bytes 7209088 | tf_op jit(solution)/shard_map/while/body/jit(_take)/gather | solution.py:29
  166.1 6.0 %fusion.25 = f32[440,440]{1,0:T(8,128)S(1)} fusion(f32[440,440]{1,0:T(8,128)S(1)} %get-tuple-element.151, bf16[32,128,440]{2,1,0:T(8,128)(2,1)} %gather_fusion, pred[32]{0:T(512)(128)(4,1)S(1)} %get-tuple-element.135, bf16[32,128,440]{2,1,0:T(8,128)(2,1)} %gather_fusion.1, pred[32]{0:T(512)(128)(4,1)S(1)} %get-tuple-element.137, ...), kind=kOutput, calls=%fused_computation.13.clone.1 | convolution fusion | flops 1591571456 | bytes 8757856 | tf_op jit(solution)/shard_map/while/body/dot_general | solution.py:32
  172.3 5.0 %gather_fusion = bf16[32,128,440]{2,1,0:T(8,128)(2,1)} fusion(bf16[32,128,440]{2,1,0:T(8,128)(2,1)} %get-tuple-element.169, s32[1024]{0:T(1024)S(1)} %pad_clamp_fusion.4), kind=kCustom, calls=%fused_computation.1.clone.clone.1 | custom fusion | bytes 7209088 | tf_op jit(solution)/shard_map/while/body/jit(_take)/gather | solution.py:30
  177.3 4.9 %gather_fusion.1 = bf16[32,128,440]{2,1,0:T(8,128)(2,1)} fusion(bf16[32,128,440]{2,1,0:T(8,128)(2,1)} %get-tuple-element.167, s32[1024]{0:T(1024)S(1)} %pad_clamp_fusion.5), kind=kCustom, calls=%fused_computation.clone.clone.1 | custom fusion | bytes 7209088 | tf_op jit(solution)/shard_map/while/body/jit(_take)/gather | solution.py:29
  182.9 6.1 %fusion.25 = f32[440,440]{1,0:T(8,128)S(1)} fusion(f32[440,440]{1,0:T(8,128)S(1)} %get-tuple-element.151, bf16[32,128,440]{2,1,0:T(8,128)(2,1)} %gather_fusion, pred[32]{0:T(512)(128)(4,1)S(1)} %get-tuple-element.135, bf16[32,128,440]{2,1,0:T(8,128)(2,1)} %gather_fusion.1, pred[32]{0:T(512)(128)(4,1)S(1)} %get-tuple-element.137, ...), kind=kOutput, calls=%fused_computation.13.clone.1 | convolution fusion | flops 1591571456 | bytes 8757856 | tf_op jit(solution)/shard_map/while/body/dot_general | solution.py:32
  188.9 22.8 %fusion = f32[112,440]{1,0:T(8,128)S(1)} fusion(f32[440,440]{1,0:T(8,128)S(1)} %get-tuple-element.49), kind=kCustom, calls=%all-reduce-scatter | all-reduce-scatter fusion | flops 197121 | bytes 972032
  211.7 2.1 collective-permute-start.3
  216.3 74.9 %all-reduce.4.cloned.1.call-done = f32[110,440]{1,0:T(8,128)} async-done(((f32[110,440]{1,0:T(8,128)}), f32[110,440]{1,0:T(8,128)}) %all-reduce.4.cloned.1.call-update) | async-done | bytes 193616 | tf_op jit(solution)/shard_map/psum | solution.py:43
  291.2 1.5 collective-permute-start
  292.7 8.5 %collective-permute-done = f32[110,440]{1,0:T(8,128)S(1)} collective-permute-done((f32[110,440]{1,0:T(8,128)}, f32[110,440]{1,0:T(8,128)S(1)}, u32[]{:S(2)}, u32[]{:S(2)}) %collective-permute-start) | collective-permute-done | bytes 193632 | tf_op jit(solution)/shard_map/ppermute | solution.py:46
  301.2 8.9 %collective-permute-done.1 = f32[110,440]{1,0:T(8,128)S(1)} collective-permute-done((f32[110,440]{1,0:T(8,128)S(1)}, f32[110,440]{1,0:T(8,128)S(1)}, u32[]{:S(2)}, u32[]{:S(2)}) %collective-permute-start.1) | collective-permute-done | bytes 193632 | tf_op jit(solution)/shard_map/ppermute | solution.py:46
  310.1 8.0 %collective-permute-done.2 = f32[110,440]{1,0:T(8,128)S(1)} collective-permute-done((f32[110,440]{1,0:T(8,128)S(1)}, f32[110,440]{1,0:T(8,128)S(1)}, u32[]{:S(2)}, u32[]{:S(2)}) %collective-permute-start.2) | collective-permute-done | bytes 193632 | tf_op jit(solution)/shard_map/ppermute | solution.py:46
  318.1 3.0 concatenate.6
  321.2 1.0 constant_dynamic-slice_fusion.1
  (40 shorter events, 5.2 us)
Async XLA Ops:
  6.5 1.6 copy-start
  6.5 107.7 %all-gather.3.cloned.1.call-start = ((), (), s32[]{:S(2)}) async-start(), calls=%async_computation | async-start | bytes 4505600 | tf_op jit(solution)/shard_map/all_gather | solution.py:16
  8.2 32.3 %copy-start.2 = (s32[1,4,440]{2,1,0:T(4,128)S(1)}, s32[1,4,440]{2,1,0:T(4,128)}, u32[]{:S(2)}) copy-start(s32[1,4,440]{2,1,0:T(4,128)} %param.16) | copy-start | bytes 21124
  8.2 32.4 %copy-start.1 = (bf16[1,4,128,440]{2,3,1,0:T(8,128)(2,1)S(1)}, bf16[1,4,128,440]{2,3,1,0:T(8,128)(2,1)}, u32[]{:S(2)}) copy-start(bf16[1,4,128,440]{2,3,1,0:T(8,128)(2,1)} %param.12) | copy-start | bytes 1351684
  40.4 108.5 %all-gather.5.cloned.1.call-start = ((), (), s32[]{:S(2)}) async-start(), calls=%async_computation.1 | async-start | bytes 4055040 | tf_op jit(solution)/shard_map/all_gather | solution.py:17
  57.4 233.8 %all-reduce.4.cloned.1.call-start = ((), (), s32[]{:S(2)}) async-start(), calls=%async_computation.2 | async-start | bytes 458752 | tf_op jit(solution)/shard_map/psum | solution.py:43
  148.9 6.6 %copy-start.3 = (s32[1,1,128]{2,1,0:T(1,128)S(1)}, s32[1,1,128]{2,1,0:T(1,128)}, u32[]{:S(2)}) copy-start(s32[1,1,128]{2,1,0:T(1,128)} %param.13) | copy-start | bytes 1540
  148.9 6.6 %copy-start.4 = (s32[1,1,128]{2,1,0:T(1,128)S(1)}, s32[1,1,128]{2,1,0:T(1,128)}, u32[]{:S(2)}) copy-start(s32[1,1,128]{2,1,0:T(1,128)} %param.14) | copy-start | bytes 1540
  155.5 58.4 %copy-start.5 = (u32[32]{0:T(128)S(1)}, u32[32]{0:T(128)}, u32[]{:S(2)}) copy-start(u32[32]{0:T(128)} %constant.127) | copy-start | bytes 388
  211.7 3.6 %collective-permute-start.3 = (f32[6,440]{1,0:T(8,128)S(1)}, f32[6,440]{1,0:T(8,128)S(1)}, u32[]{:S(2)}, u32[]{:S(2)}) collective-permute-start(f32[6,440]{1,0:T(8,128)S(1)} %slice.8), channel_id=1, source_target_pairs={{0,1},{1,2},{2,3},{4,5},{5,6},{6,7},{8,9},{9,10},{10,11},{12,13},{... | collective-permute-start | bytes 31688
  291.2 10.0 %collective-permute-start = (f32[110,440]{1,0:T(8,128)}, f32[110,440]{1,0:T(8,128)S(1)}, u32[]{:S(2)}, u32[]{:S(2)}) collective-permute-start(f32[110,440]{1,0:T(8,128)} %all-reduce.4.cloned.1.call-done), channel_id=1, source_target_pairs={{0,1},{1,2},{2,3},{3,0},{4,5},{5,6},{6,7},{7,4},{8,9},{9,10},{10,1... | collective-permute-start | bytes 580808 | tf_op jit(solution)/shard_map/ppermute | solution.py:46
  301.2 8.9 %collective-permute-start.1 = (f32[110,440]{1,0:T(8,128)S(1)}, f32[110,440]{1,0:T(8,128)S(1)}, u32[]{:S(2)}, u32[]{:S(2)}) collective-permute-start(f32[110,440]{1,0:T(8,128)S(1)} %collective-permute-done), channel_id=1, source_target_pairs={{0,1},{1,2},{2,3},{3,0},{4,5},{5,6},{6,7},{7,4},{8,9},{9,10},{10,1... | collective-permute-start | bytes 580808 | tf_op jit(solution)/shard_map/ppermute | solution.py:46
  310.1 8.0 %collective-permute-start.2 = (f32[110,440]{1,0:T(8,128)S(1)}, f32[110,440]{1,0:T(8,128)S(1)}, u32[]{:S(2)}, u32[]{:S(2)}) collective-permute-start(f32[110,440]{1,0:T(8,128)S(1)} %collective-permute-done.1), channel_id=1, source_target_pairs={{0,1},{1,2},{2,3},{3,0},{4,5},{5,6},{6,7},{7,4},{8,9},{9,10},{10,1... | collective-permute-start | bytes 580808 | tf_op jit(solution)/shard_map/ppermute | solution.py:46
Sparse Core Ops, SparseCore 0:
  40.5 73.7 all-gather.2
  116.2 32.6 all-gather.4
  216.4 74.7 all-reduce.3
